TPU v7x, 512 devices: a whole 4x4x16 slice. The times are simulated.
512 devices in a mesh: expert: 128 (over z, y_hi, x), half: 4 (over y_lo, core).
Axes of the slice: x: 4, y: 4 (y_hi: 2, y_lo: 2; y = y_hi * 2 + y_lo), z: 16, core: 2. Of those that a mesh axis runs over, the one named last changes fastest.
Arguments:
- tokens: bfloat16 [131072, 1024], P(('expert', 'half')), may hold values from -6 to 6
- router: bfloat16 [1024, 256], replicated, may hold values from -1 to 1
- w_in: bfloat16 [128, 1024, 3072], P('expert', None, 'half'), may hold values from -0.1875 to 0.1875
- w_out: bfloat16 [128, 3072, 1024], P('expert', 'half'), may hold values from -0.109375 to 0.109375
Outputs:
- mixed: bfloat16 [131072, 1024], P(('expert', 'half'))
All inputs are finite; a program needn't handle non-finite values.
Results may differ from a plain program's by a relative error of at most 0.018.
Values may be sent and summed in bfloat16 or wider, within the bound.
No kernel may reach another device: no remote copies, remote signals or barrier semaphores. Data moves between devices by JAX's collectives and lax.ppermute only.
A program may use at most 64 MiB of HBM per device.

v0:
```python
import jax
import jax.numpy as jnp
from jax import lax
from jax.sharding import PartitionSpec as P

SLOTS = 2
PATCHES = 256


def from_everyone(value, axis):
    length = lax.axis_size(axis)
    return lax.all_to_all(
        jnp.broadcast_to(value[None], (length, *value.shape)), axis, 0, 0, tiled=True
    )


def in_order(parts, dim):
    parts = jnp.moveaxis(parts, 0, dim)
    dims = parts.shape
    return parts.reshape(*dims[:dim], dims[dim] * dims[dim + 1], *dims[dim + 2 :])


def gathered_copies(value, axis, dim):
    parts = from_everyone(value, axis)
    return in_order(parts, dim)


def cut_along(value, dim, length):
    before, after = (value.shape[:dim], value.shape[dim + 1 :])
    return jnp.moveaxis(value.reshape(*before, length, -1, *after), dim, 0)


def summed_on_arrival(value, axis, dim):
    parts = cut_along(value, dim, lax.axis_size(axis))
    arrived = lax.all_to_all(parts, axis, split_axis=0, concat_axis=0, tiled=True)
    return arrived.astype(jnp.float32).sum(axis=0)


def expert_quarter(rows, first, second):
    hidden = jax.nn.gelu(
        jnp.einsum("erd,edf->erf", rows, first, preferred_element_type=jnp.float32)
    ).astype(jnp.bfloat16)
    return jnp.einsum("erf,efd->erd", hidden, second, preferred_element_type=jnp.float32)


def on_device(tokens, router, w_in, w_out):
    width = tokens.shape[1]
    images = tokens.shape[0] // PATCHES
    experts_all = router.shape[1] // SLOTS
    picture = tokens.reshape(images, PATCHES, width)
    logits = jnp.einsum("imd,dc->imc", picture, router, preferred_element_type=jnp.float32)
    dispatch = jax.nn.softmax(logits, axis=1).astype(jnp.bfloat16)
    combine = jax.nn.softmax(logits, axis=2).astype(jnp.bfloat16)
    slot_input = jnp.einsum(
        "imc,imd->icd", dispatch, picture, preferred_element_type=jnp.float32
    ).astype(jnp.bfloat16)
    outgoing = slot_input.reshape(images, experts_all, SLOTS, width)
    arrived = lax.all_to_all(outgoing, "expert", split_axis=1, concat_axis=0, tiled=True)
    local_experts = arrived.shape[1]
    slot_rows_local = jnp.transpose(arrived, (1, 0, 2, 3)).reshape(local_experts, -1, width)
    terms = expert_quarter(gathered_copies(slot_rows_local, "half", 1), w_in, w_out)
    result = summed_on_arrival(terms.astype(jnp.bfloat16), "half", 1)
    back = jnp.transpose(
        result.astype(jnp.bfloat16).reshape(local_experts, -1, SLOTS, width), (1, 0, 2, 3)
    )
    returned = lax.all_to_all(back, "expert", split_axis=0, concat_axis=1, tiled=True)
    slot_output = returned.reshape(images, experts_all * SLOTS, width)
    mixed = jnp.einsum(
        "imc,icd->imd", combine, slot_output, preferred_element_type=jnp.float32
    ).astype(jnp.bfloat16)
    return mixed.reshape(-1, width)


def solution(mesh):
    return jax.shard_map(
        on_device,
        mesh=mesh,
        in_specs=(
            P(("expert", "half"), None),
            P(),
            P("expert", None, "half"),
            P("expert", "half", None),
        ),
        out_specs=P(("expert", "half"), None),
        check_vma=False,
    )
```

profile of v0, /device:TPU:32, one launch (start us, length us, event | category | flops | bytes accessed | tf_op | source)
XLA Modules:
  0.0 171.6 jit_solution(13309101023838386148)
XLA Ops:
  0.0 0.0 copy-start
  0.0 1.7 fusion.30
  1.7 0.2 fusion.20
  1.9 1.4 convolution_convert_fusion.2
  3.3 0.2 reshape.92
  3.5 56.3 %all_to_all.28 = bf16[1,128,2,1024]{3,2,0,1:T(2,128)(2,1)S(1)} all-to-all(bf16[1,128,2,1024]{3,2,0,1:T(2,128)(2,1)S(1)} %bitcast.24), channel_id=1, replica_groups=mesh['expert'=128,'half'=4] {'expert'}, dimensions={1} | all-to-all | bytes 1048576 | tf_op jit(solution)/shard_map/all_to_all | solution.py:58
  59.8 0.2 broadcast_in_dim.4
  60.0 0.3 broadcast_in_dim.5
  60.3 0.0 copy-start.1
  60.3 29.0 %all_to_all.29 = bf16[4,1,256,1024]{3,2,1,0:T(8,128)(2,1)} all-to-all(bf16[4,1,256,1024]{3,2,1,0:T(8,128)(2,1)S(1)} %broadcast_in_dim.5), channel_id=1, replica_groups=mesh['expert'=128,'half'=4] {'half'}, dimensions={0} | all-to-all | bytes 4194304 | tf_op jit(solution)/shard_map/all_to_all | solution.py:12
  89.3 0.0 copy-done
  89.3 0.0 copy-done.1
  89.3 7.4 %convolution_convert_fusion = bf16[1024,1024]{1,0:T(8,128)(2,1)} fusion(bf16[1,768,1024]{2,1,0:T(8,128)(2,1)S(1)} %copy-done, bf16[1024,1024]{1,0:T(8,128)(2,1)} %bitcast.22, bf16[1,1024,768]{2,1,0:T(8,128)(2,1)S(1)} %copy-done.1), kind=kOutput, calls=%fused_computation.9 | convolution fusion | flops 3229351936 | bytes 7340032 | tf_op jit(solution)/shard_map/erf,efd->erd/dot_general | solution.py:43
  96.8 30.1 %all_to_all.30 = bf16[4,1,256,1024]{3,2,1,0:T(8,128)(2,1)} all-to-all(bf16[4,1,256,1024]{3,2,1,0:T(8,128)(2,1)} %bitcast.23), channel_id=1, replica_groups=mesh['expert'=128,'half'=4] {'half'}, dimensions={0} | all-to-all | bytes 4194304 | tf_op jit(solution)/shard_map/all_to_all | solution.py:35
  126.9 2.0 %reduce_sum.32 = bf16[256,1024]{1,0:T(8,128)(2,1)S(1)} reduce(bf16[4,1,256,1024]{3,2,1,0:T(8,128)(2,1)} %all_to_all.30, bf16[]{:T(256)} %constant.14.clone.1), dimensions={0,1}, to_apply=%region_4.0 | reduce | flops 786432 | bytes 2621442 | tf_op jit(solution)/shard_map/reduce_sum | solution.py:36
  128.9 0.2 transpose_reshape.7
  129.1 41.1 %all_to_all.31 = bf16[128,1,2,1024]{3,2,1,0:T(2,128)(2,1)S(1)} all-to-all(bf16[128,1,2,1024]{3,2,1,0:T(2,128)(2,1)S(1)} %transpose_reshape.7), channel_id=1, replica_groups=mesh['expert'=128,'half'=4] {'expert'}, dimensions={0} | all-to-all | bytes 1048576 | tf_op jit(solution)/shard_map/all_to_all | solution.py:66
  170.3 0.2 reshape.96
  170.5 1.2 convolution_convert_fusion.1
Async XLA Ops:
  0.0 89.3 %copy-start = (bf16[1,768,1024]{2,1,0:T(8,128)(2,1)S(1)}, bf16[1,768,1024]{2,1,0:T(8,128)(2,1)}, u32[]{:S(2)}) copy-start(bf16[1,768,1024]{2,1,0:T(8,128)(2,1)} %param.7) | copy-start | bytes 4718596
  60.3 29.1 %copy-start.1 = (bf16[1,1024,768]{2,1,0:T(8,128)(2,1)S(1)}, bf16[1,1024,768]{2,1,0:T(8,128)(2,1)}, u32[]{:S(2)}) copy-start(bf16[1,1024,768]{2,1,0:T(8,128)(2,1)} %param.6) | copy-start | bytes 4718596
where the time goes:
time: 172 us
  blocking collectives  157 us (91%)
  matrix products  11.7 us (7%)
  other arithmetic  2.22 us (1%)
    all_to_all x1, blocking collectives, on_device(): lax.all_to_all(outgoing, 'expert', split_axis=1, concat_axis=0, tiled=True)  56.3 us
    all_to_all x1, blocking collectives, on_device(): lax.all_to_all(back, 'expert', split_axis=0, concat_axis=1, tiled=True)  41.1 us
    all_to_all x1, blocking collectives, summed_on_arrival(): lax.all_to_all(parts, axis, split_axis=0, concat_axis=0, tiled=True)  30.1 us
    all_to_all x1, blocking collectives, from_everyone(): lax.all_to_all(jnp.broadcast_to(value[None], (length, *value.shape)), axi...  29 us
    dot_general x1, matrix products, expert_quarter(): jnp.einsum('erf,efd->erd', hidden, second, preferred_element_type=jnp.flo...  7.43 us

commit v1 on v0

--- a/solution.py
+++ b/solution.py
@@ -1,3 +1,4 @@
+import functools
 import jax
 import jax.numpy as jnp
 from jax import lax
@@ -5,6 +6,17 @@
 
 SLOTS = 2
 PATCHES = 256
+
+
+def touch_the_array(u, shard_axis):
+    block_out = jax.lax.axis_size(shard_axis)
+    x_next = jnp.split(u, block_out, 1)
+    left_arr = jnp.stack(x_next, 0)
+    z2 = jax.lax.all_to_all(left_arr, shard_axis, 0, 0)
+    return jnp.concatenate(z2, 0)
+
+
+advance_pipes = functools.partial(touch_the_array, shard_axis="expert")
 
 
 def from_everyone(value, axis):
@@ -55,7 +67,7 @@
         "imc,imd->icd", dispatch, picture, preferred_element_type=jnp.float32
     ).astype(jnp.bfloat16)
     outgoing = slot_input.reshape(images, experts_all, SLOTS, width)
-    arrived = lax.all_to_all(outgoing, "expert", split_axis=1, concat_axis=0, tiled=True)
+    arrived = advance_pipes(outgoing)
     local_experts = arrived.shape[1]
     slot_rows_local = jnp.transpose(arrived, (1, 0, 2, 3)).reshape(local_experts, -1, width)
     terms = expert_quarter(gathered_copies(slot_rows_local, "half", 1), w_in, w_out)

time: 172 us -> 174 us (1.012)
  no operation moved by 1% of the time
where the time goes in v1:
time: 174 us
  blocking collectives  156 us (90%)
  matrix products  12.1 us (7%)
  local copies, waits for them, and re-layouts  2.67 us (2%)
  other arithmetic  2.22 us (1%)
    all_to_all x1, blocking collectives, touch_the_array(): z2 = jax.lax.all_to_all(left_arr, shard_axis, 0, 0)  56.3 us
    all_to_all x1, blocking collectives, on_device(): lax.all_to_all(back, 'expert', split_axis=0, concat_axis=1, tiled=True)  41.2 us
    all_to_all x1, blocking collectives, summed_on_arrival(): lax.all_to_all(parts, axis, split_axis=0, concat_axis=0, tiled=True)  30.1 us
    all_to_all x1, blocking collectives, from_everyone(): lax.all_to_all(jnp.broadcast_to(value[None], (length, *value.shape)), axi...  28.9 us
    dot_general x1, matrix products, expert_quarter(): jnp.einsum('erf,efd->erd', hidden, second, preferred_element_type=jnp.flo...  7.86 us

profile of v1, /device:TPU:32, one launch (start us, length us, event | category | flops | bytes accessed | tf_op | source)
XLA Modules:
  0.0 173.9 jit_solution(11573361656570206778)
XLA Ops:
  0.0 0.0 copy-start
  0.0 1.7 fusion.30
  1.7 0.2 fusion.20
  1.9 1.4 convolution_convert_fusion.2
  3.3 0.2 reshape.88
  5.5 56.3 %all_to_all.24 = bf16[128,1,1,2,1024]{4,3,2,1,0:T(2,128)(2,1)S(1)} all-to-all(bf16[128,1,1,2,1024]{4,3,2,1,0:T(2,128)(2,1)S(1)} %constant_dynamic-update-slice_fusion), channel_id=1, replica_groups=mesh['expert'=128,'half'=4] {'expert'}, dimensions={0} | all-to-all | bytes 1048576 | tf_op jit(solution)/shard_map/all_to_all | solution.py:15
  61.8 0.2 broadcast_in_dim.4
  62.0 0.3 broadcast_in_dim.5
  62.3 28.9 %all_to_all.25 = bf16[4,1,256,1024]{3,2,1,0:T(8,128)(2,1)} all-to-all(bf16[4,1,256,1024]{3,2,1,0:T(8,128)(2,1)S(1)} %broadcast_in_dim.5), channel_id=1, replica_groups=mesh['expert'=128,'half'=4] {'half'}, dimensions={0} | all-to-all | bytes 4194304 | tf_op jit(solution)/shard_map/all_to_all | solution.py:24
  91.2 0.0 copy-done
  91.2 7.9 %convolution_convert_fusion = bf16[1024,1024]{1,0:T(8,128)(2,1)} fusion(bf16[1,768,1024]{2,1,0:T(8,128)(2,1)S(1)} %copy-done, bf16[1024,1024]{1,0:T(8,128)(2,1)} %bitcast.531, bf16[1,1024,768]{2,1,0:T(8,128)(2,1)} %param.6), kind=kOutput, calls=%fused_computation.9 | convolution fusion | flops 3229351936 | bytes 7340032 | tf_op jit(solution)/shard_map/erf,efd->erd/dot_general | solution.py:55
  99.0 30.1 %all_to_all.26 = bf16[4,1,256,1024]{3,2,1,0:T(8,128)(2,1)} all-to-all(bf16[4,1,256,1024]{3,2,1,0:T(8,128)(2,1)} %bitcast.532), channel_id=1, replica_groups=mesh['expert'=128,'half'=4] {'half'}, dimensions={0} | all-to-all | bytes 4194304 | tf_op jit(solution)/shard_map/all_to_all | solution.py:47
  129.2 2.0 %reduce_sum.32 = bf16[256,1024]{1,0:T(8,128)(2,1)S(1)} reduce(bf16[4,1,256,1024]{3,2,1,0:T(8,128)(2,1)} %all_to_all.26, bf16[]{:T(256)} %constant.14.clone.1), dimensions={0,1}, to_apply=%region_4.0 | reduce | flops 786432 | bytes 2621442 | tf_op jit(solution)/shard_map/reduce_sum | solution.py:48
  131.2 0.2 transpose_reshape.7
  131.4 41.2 %all_to_all.27 = bf16[128,1,2,1024]{3,2,1,0:T(2,128)(2,1)S(1)} all-to-all(bf16[128,1,2,1024]{3,2,1,0:T(2,128)(2,1)S(1)} %transpose_reshape.7), channel_id=1, replica_groups=mesh['expert'=128,'half'=4] {'expert'}, dimensions={0} | all-to-all | bytes 1048576 | tf_op jit(solution)/shard_map/all_to_all | solution.py:78
  172.5 0.2 reshape.92
  172.7 1.2 convolution_convert_fusion.1
  (128 shorter events, 1.6 us)
Async XLA Ops:
  0.0 91.2 %copy-start = (bf16[1,768,1024]{2,1,0:T(8,128)(2,1)S(1)}, bf16[1,768,1024]{2,1,0:T(8,128)(2,1)}, u32[]{:S(2)}) copy-start(bf16[1,768,1024]{2,1,0:T(8,128)(2,1)} %param.7) | copy-start | bytes 4718596
